TPU v7x, 32 devices: a whole 2x2x4 slice. The times are simulated.
32 devices in a mesh: ka: 8 (over z, x), ga: 4 (over y, core).
Axes of the slice: x: 2, y: 2, z: 4, core: 2. Of those that a mesh axis runs over, the one named last changes fastest.
Arguments:
- coefficients: bfloat16 [8, 2, 256, 55296], P('ka', None, 'ga'), may hold values from -0.4375 to 0.4375
- shift_map: int32 [8, 3, 55296], P('ka', None, 'ga'), may hold values from 0 to 55295, as said below
- phase_angle: float32 [8, 3], P('ka'), may hold values from -3.140625 to 3.140625
Outputs:
- intersections: float32 [8, 3, 2, 256, 256], P('ka', None, None, 'ga')
Inputs may be any that keep to these rules, and one draw needn't show every extreme that they name: Each aligned block of 13824 consecutive entries of shift_map[k, b] is a permutation of the indices of that same block; it maps aligned tiles of 128 entries onto aligned tiles of 128 indices.
All inputs are finite; a program needn't handle non-finite values.
Results may differ from a plain program's by a relative error of at most 0.0003.
Values may be sent and summed in bfloat16 or wider, within the bound.
A program may use at most 192 MiB of HBM per device.

v0:
```python
import functools

import jax
import jax.numpy as jnp
from jax import lax
from jax.experimental import pallas as pl
from jax.experimental.pallas import tpu as pltpu
from jax.sharding import PartitionSpec as P


LANES = 128
UNROLL = 6
F32 = jnp.float32
NT = (((1,), (1,)), ((), ()))


def passed_along(value, axis, steps):
    count = lax.axis_size(axis)
    pairs = [(source, (source + steps) % count) for source in range(count)]
    return lax.ppermute(value, axis, pairs)


def swapped(block, axis, bit):
    count = lax.axis_size(axis)
    route = []
    for low in range(count):
        high = low | 1 << bit
        if high != low and high < count:
            route += [(low, high), (high, low)]
    return lax.ppermute(block, axis, route)


def cross_terms(left, moved):
    prods = jnp.einsum("amg,bng->abmn", left, moved, preferred_element_type=jnp.float32)
    real_part = prods[0, 0] + prods[1, 1]
    imag_part = prods[0, 1] - prods[1, 0]
    return jnp.stack([real_part, imag_part])


def rotated_by(phase, real_part, imag_part):
    cosine = jnp.cos(phase)[:, None, None]
    sine = jnp.sin(phase)[:, None, None]
    return jnp.stack(
        [cosine * real_part - sine * imag_part, sine * real_part + cosine * imag_part], axis=1
    )


def general(coefficients, shift_map, phase_angle):
    own = lax.all_to_all(coefficients, "ga", split_axis=3, concat_axis=2, tiled=True)
    next_x = passed_along(own, "ka", -4)
    next_y = swapped(own, "ka", 1)
    next_z = swapped(own, "ka", 0)
    block_width = own.shape[3]
    local_map = shift_map[0] - lax.axis_index("ga") * block_width
    left = own[0]
    movers = []
    for direction, other in enumerate((next_x, next_y, next_z)):
        movers.append(jnp.take(other[0], local_map[direction], axis=2))
    parts = jnp.stack([cross_terms(left, moved) for moved in movers])
    summed = lax.psum_scatter(
        jnp.transpose(parts, (2, 0, 1, 3)), "ga", scatter_dimension=0, tiled=True
    )
    summed = jnp.transpose(summed, (1, 2, 0, 3))
    return rotated_by(phase_angle[0], summed[:, 0], summed[:, 1])[None]


def largest_divisor(count, most):
    return max(d for d in range(1, most + 1) if count % d == 0)


def copy_body(index, source, target):
    target[...] = source[...]


def block_of(source, index, width):
    parts, rows, _ = source.shape
    per = largest_divisor(width // LANES, 36)
    cols, steps = per * LANES, width // (per * LANES)
    grid_spec = pltpu.PrefetchScalarGridSpec(
        num_scalar_prefetch=1,
        grid=(steps,),
        in_specs=[pl.BlockSpec((parts, rows, cols), lambda i, at: (0, 0, at[0] * steps + i))],
        out_specs=pl.BlockSpec((parts, rows, cols), lambda i, at: (0, 0, i)),
    )
    return pl.pallas_call(
        copy_body,
        grid_spec=grid_spec,
        out_shape=jax.ShapeDtypeStruct((parts, rows, width), source.dtype),
        cost_estimate=pl.CostEstimate(flops=0, bytes_accessed=4 * parts * rows * width, transcendentals=0),
    )(index.reshape(1), source)


def pair_body(unroll, tile1, tile2, *refs):
    pieces = refs[:4]
    others = refs[4:-5]
    rows1, rows2, near_ref, far_ref, acc = refs[-5:]
    step = pl.program_id(0)
    iota = lax.broadcasted_iota(jnp.int32, (LANES, LANES), 0)

    def tile_of(s):
        at = pl.ds(pl.multiple_of(s * LANES, LANES), LANES)
        value = others[0][:, at]
        for other in others[1:]:
            value = value + other[:, at]
        return value

    columns = []
    for i in range(unroll):
        t = step * unroll + i
        s1, s2 = tile1[t], tile2[t]
        pick1 = jnp.where(iota == rows1[pl.ds(t, 1), :], 1.0, 0.0).astype(jnp.bfloat16)
        pick2 = jnp.where(iota == rows2[pl.ds(s2, 1), :], 1.0, 0.0).astype(jnp.bfloat16)
        g1 = jnp.dot(tile_of(s1), pick1, preferred_element_type=F32).astype(jnp.bfloat16)
        g2 = lax.dot_general(tile_of(s2), pick2, NT, preferred_element_type=F32).astype(jnp.bfloat16)
        columns.append(jnp.concatenate([g1, g2], axis=0))
    right = jnp.concatenate(columns, axis=1)
    left = jnp.concatenate([piece[...] for piece in pieces], axis=0)
    term = lax.dot_general(left, right, NT, preferred_element_type=F32)

    @pl.when(step == 0)
    def _():
        acc[...] = term

    @pl.when(step > 0)
    def _():
        acc[...] += term

    @pl.when(step == pl.num_programs(0) - 1)
    def _():
        nb = others[0].shape[0] // 2
        mb = pieces[0].shape[0] // 2
        for r in range(4):
            re = acc[2 * r * mb : (2 * r + 1) * mb, :]
            im = acc[(2 * r + 1) * mb : (2 * r + 2) * mb, :]
            near_ref[r, 0] = re[:, :nb] + im[:, nb : 2 * nb]
            near_ref[r, 1] = re[:, nb : 2 * nb] - im[:, :nb]
            far_ref[r, 0] = (re[:, 2 * nb : 3 * nb] + im[:, 3 * nb :]).T
            far_ref[r, 1] = (im[:, 2 * nb : 3 * nb] - re[:, 3 * nb :]).T


def pair_products(pieces, others, tile1, tile2, rows1, rows2):
    _, mb, width = pieces[0].shape
    nb = others[0].shape[1]
    tiles = width // LANES
    unroll = largest_divisor(tiles, UNROLL)
    flat = [piece.reshape(2 * mb, width) for piece in pieces]
    flat_others = [other.reshape(2 * nb, width) for other in others]
    whole = lambda shape: pl.BlockSpec(shape, lambda i, *_: (0,) * len(shape))
    grid_spec = pltpu.PrefetchScalarGridSpec(
        num_scalar_prefetch=2,
        grid=(tiles // unroll,),
        in_specs=[pl.BlockSpec((2 * mb, unroll * LANES), lambda i, *_: (0, i))] * 4
        + [whole((2 * nb, width))] * len(others)
        + [whole((tiles, LANES)), whole((tiles, LANES))],
        out_specs=[whole((4, 2, mb, nb)), whole((4, 2, nb, mb))],
        scratch_shapes=[pltpu.VMEM((8 * mb, 4 * nb), F32)],
    )
    return pl.pallas_call(
        functools.partial(pair_body, unroll),
        grid_spec=grid_spec,
        out_shape=[
            jax.ShapeDtypeStruct((4, 2, mb, nb), F32),
            jax.ShapeDtypeStruct((4, 2, nb, mb), F32),
        ],
        cost_estimate=pl.CostEstimate(
            flops=160 * mb * nb * width, bytes_accessed=(16 * mb + 4 * nb) * width, transcendentals=0
        ),
    )(tile1, tile2, *flat, *flat_others, rows1, rows2)


def paired(coefficients, shift_map, phase_angle):
    return paired_points(coefficients, shift_map, phase_angle)


def paired_points(coefficients, shift_map, phase_angle):
    raw = coefficients[0]
    k = lax.axis_index("ka")
    j = lax.axis_index("ga")
    points, group = lax.axis_size("ka"), lax.axis_size("ga")
    half = group // 2
    width = shift_map.shape[2]
    tiles = width // LANES
    parity_of = lambda point: (point ^ (point >> 1) ^ (point >> 2)) & 1
    parity = parity_of(k)
    mine = parity * half + j // 2
    theirs = (1 - parity) * half + j // 2
    flips = (4, 2, 1)
    mates = lambda value, mask: lax.ppermute(value, "ga", [(s, s ^ mask) for s in range(group)])
    both = lambda value, pairs: lax.ppermute(value, ("ka", "ga"), pairs)
    middle = [(s, s ^ 6) for s in range(points) if (s >> 1) in (1, 2)]
    outward = [(s, s ^ 2) for s in range(points) if (s >> 1) in (1, 2)]
    hop = lambda value, b: lax.ppermute(value, "ka", [(s, s ^ flips[b]) for s in range(points)])
    along = lambda value, pairs: lax.ppermute(value, "ka", pairs)

    maps = shift_map[0]
    arrived = [
        both(
            value,
            [
                ((p ^ flip) * group + parity_of(p) * half + y, p * group + 2 * y)
                for p in range(points)
                for y in range(half)
            ],
        )
        for value, flip in [(maps, 0)] + [(maps[b : b + 1], flips[b]) for b in range(3)]
    ]
    out_own = block_of(raw, theirs, width)
    out_own, *arrived = lax.optimization_barrier((out_own, *arrived))
    arrived = jnp.concatenate(arrived, axis=0)
    arrived = jnp.where(j % 2 == 0, arrived, mates(arrived, 1)) - mine * width

    first1 = hop(out_own, 1)
    parked0 = along(out_own, middle)
    relay_at, out_own = lax.optimization_barrier((theirs ^ 1, out_own))
    out_relay = block_of(raw, relay_at, width)
    relay = mates(out_relay, 2)
    first2 = hop(out_own, 2)
    piece0 = block_of(raw, mine, width)
    piece1 = mates(piece0, 1)
    first0 = [along(first1, middle)]
    first0 += [along(parked0, outward)]
    second1 = hop(relay, 1)
    parked1 = along(relay, middle)
    second2 = hop(relay, 2)
    give = block_of(raw, mine ^ 1, width)
    give, relay = lax.optimization_barrier((give, relay))
    piece2 = mates(give, 2)
    piece3 = mates(piece2, 1)
    pieces = [piece0, piece1, piece2, piece3]
    second0 = [along(second1, middle)]
    second0 += [along(parked1, outward)]
    early = [first0, [first1], [first2]]
    late = [second0, [second1], [second2]]

    tables = []
    place = jnp.arange(tiles, dtype=jnp.int32)
    for b in range(3):
        to_other = arrived[b].reshape(tiles, LANES)
        to_mine = arrived[3 + b].reshape(tiles, LANES)
        tile1 = to_other[:, 0] // LANES
        tile_of = to_mine[:, 0] // LANES
        tile2 = jnp.sum(jnp.where(tile_of[None, :] == place[:, None], place[None, :], 0), axis=1)
        tables.append((tile1, tile2, to_other % LANES, to_mine % LANES))

    sums = [None] * 3
    for b, which in ((2, 0), (2, 1), (1, 0), (1, 1), (0, 0), (0, 1)):
        near, far = pair_products(pieces, (early, late)[which][b], *tables[b])
        mask = 2 * which
        far = both(
            far,
            [
                (p * group + s, (p ^ flips[b]) * group + (s ^ mask))
                for p in range(points)
                for s in range(group)
            ],
        )
        got = [near[0]] + [mates(near[r], r) for r in (1, 2, 3)]
        term = [far[t ^ mask] + got[t ^ mask] for t in range(4)]
        sums[b] = term if sums[b] is None else [x + y for x, y in zip(sums[b], term)]
    stacked = jnp.stack([jnp.stack(one) for one in sums], axis=1)
    ordered = [lax.dynamic_index_in_dim(stacked, j ^ q, 0, keepdims=False) for q in range(4)]
    summed = jnp.concatenate(ordered, axis=-1)
    return rotated_by(phase_angle[0], summed[:, 0], summed[:, 1])[None]


def solution(mesh):
    in_specs = (P("ka", None, "ga", None), P("ka", None, "ga"), P("ka", None))
    out_specs = P("ka", None, None, "ga", None)
    both_ways = mesh.shape["ka"] == 8 and mesh.shape["ga"] == 4
    local = paired if both_ways else general
    return jax.shard_map(local, mesh=mesh, in_specs=in_specs, out_specs=out_specs, check_vma=False)
```

profile of v0, /device:TPU:0, one launch (start us, length us, event | category | flops | bytes accessed | tf_op | source)
XLA Modules:
  0.0 511.9 jit_solution(9605010739978410451)
XLA Ops:
  0.0 1.0 copy.6
  1.7 0.9 slice_bitcast_fusion.36
  2.5 1.3 collective-permute-start.1
  3.8 1.3 collective-permute-start.2
  5.1 1.3 collective-permute-start.3
  6.5 4.7 shard_map.37
  11.3 2.9 collective-permute-done.2
  14.1 1.8 collective-permute-done.3
  16.0 4.8 shard_map.40
  20.8 4.3 collective-permute-start.6
  25.1 4.7 shard_map.38
  29.8 5.1 shard_map.39
  34.9 1.7 collective-permute-start.9
  36.6 64.6 %collective-permute-done.6 = bf16[2,64,13824]{2,1,0:T(8,128)(2,1)} collective-permute-done((bf16[2,64,13824]{2,1,0:T(8,128)(2,1)}, bf16[2,64,13824]{2,1,0:T(8,128)(2,1)}, u32[]{:S(2)}, u32[]{:S(2)}) %collective-permute-start.6) | collective-permute-done | bytes 3538976 | tf_op jit(solution)/shard_map/ppermute | solution.py:188
  101.2 1.7 collective-permute-start.7
  102.9 2.0 pad_add_fusion
  104.9 2.5 collective-permute-start.11
  107.4 0.8 collective-permute-start.35
  108.3 2.3 collective-permute-start.14
  110.6 3.8 collective-permute-done.9
  114.4 2.4 collective-permute-start.16
  116.8 61.6 %collective-permute-done.7 = bf16[2,64,13824]{2,1,0:T(8,128)(2,1)} collective-permute-done((bf16[2,64,13824]{2,1,0:T(8,128)(2,1)}, bf16[2,64,13824]{2,1,0:T(8,128)(2,1)}, u32[]{:S(2)}, u32[]{:S(2)}) %collective-permute-start.7) | collective-permute-done | bytes 3538976 | tf_op jit(solution)/shard_map/ppermute | solution.py:188
  178.4 1.2 select_subtract_fusion
  179.7 0.9 slice_reduce_fusion.10
  180.7 3.2 collective-permute-start.33
  184.6 0.7 select_reduce_fusion.tile2
  190.2 2.5 collective-permute-start.10
  192.7 1.3 collective-permute-start.12
  194.0 2.4 collective-permute-start.15
  196.4 1.5 collective-permute-start.17
  197.9 21.2 %shard_map.46 = (f32[4,2,64,64]{3,2,1,0:T(8,128)}, f32[4,2,64,64]{3,2,1,0:T(8,128)}) custom-call(s32[108]{0:T(128)} %get-tuple-element.93.tile1, s32[108]{0:T(128)} %select_reduce_fusion.tile2, bf16[128,13824]{1,0:T(8,128)(2,1)} %bitcast.278, bf16[128,13824]{1,0:T(8,128)(2,1)} %bitcast.8.refs_1_, bf16[128,13824]{1,0:T(8,128)(2,1)} %bitcast.11.refs_2_, ...), custom_call_target="tpu_custom_call" | custom-call | flops 9059696640 | bytes 17694720 | tf_op jit(solution)/shard_map/pallas_call | solution.py:158
  219.1 1.6 slice_bitcast_fusion.23
  220.7 42.0 %collective-permute-done.33 = bf16[2,64,13824]{2,1,0:T(8,128)(2,1)} collective-permute-done((bf16[2,64,13824]{2,1,0:T(8,128)(2,1)S(1)}, bf16[2,64,13824]{2,1,0:T(8,128)(2,1)}, u32[]{:S(2)}, u32[]{:S(2)}) %collective-permute-start.33) | collective-permute-done | bytes 3538976 | tf_op jit(solution)/shard_map/ppermute | solution.py:192
  262.9 21.2 %shard_map.45 = (f32[4,2,64,64]{3,2,1,0:T(8,128)}, f32[4,2,64,64]{3,2,1,0:T(8,128)}) custom-call(s32[108]{0:T(128)} %get-tuple-element.93.tile1, s32[108]{0:T(128)} %select_reduce_fusion.tile2, bf16[128,13824]{1,0:T(8,128)(2,1)} %bitcast.279, bf16[128,13824]{1,0:T(8,128)(2,1)} %bitcast.8.refs_1_, bf16[128,13824]{1,0:T(8,128)(2,1)} %bitcast.11.refs_2_, ...), custom_call_target="tpu_custom_call" | custom-call | flops 9059696640 | bytes 17694720 | tf_op jit(solution)/shard_map/pallas_call | solution.py:158
  284.1 0.9 slice_bitcast_fusion.22
  285.0 21.2 %shard_map.44 = (f32[4,2,64,64]{3,2,1,0:T(8,128)}, f32[4,2,64,64]{3,2,1,0:T(8,128)}) custom-call(s32[108]{0:T(128)} %get-tuple-element.95.tile1, s32[108]{0:T(128)} %select_reduce_fusion.1.tile2, bf16[128,13824]{1,0:T(8,128)(2,1)} %bitcast.280, bf16[128,13824]{1,0:T(8,128)(2,1)} %bitcast.8.refs_1_, bf16[128,13824]{1,0:T(8,128)(2,1)} %bitcast.11.refs_2_, ...), custom_call_target="tpu_custom_call" | custom-call | flops 9059696640 | bytes 17694720 | tf_op jit(solution)/shard_map/pallas_call | solution.py:158
  306.2 0.9 slice_bitcast_fusion.29
  307.1 21.3 %shard_map.43 = (f32[4,2,64,64]{3,2,1,0:T(8,128)}, f32[4,2,64,64]{3,2,1,0:T(8,128)}) custom-call(s32[108]{0:T(128)} %get-tuple-element.95.tile1, s32[108]{0:T(128)} %select_reduce_fusion.1.tile2, bf16[128,13824]{1,0:T(8,128)(2,1)} %bitcast.281, bf16[128,13824]{1,0:T(8,128)(2,1)} %bitcast.8.refs_1_, bf16[128,13824]{1,0:T(8,128)(2,1)} %bitcast.11.refs_2_, ...), custom_call_target="tpu_custom_call" | custom-call | flops 9059696640 | bytes 17694720 | tf_op jit(solution)/shard_map/pallas_call | solution.py:158
  328.5 22.5 %collective-permute-done.17 = bf16[2,64,13824]{2,1,0:T(8,128)(2,1)} collective-permute-done((bf16[2,64,13824]{2,1,0:T(8,128)(2,1)}, bf16[2,64,13824]{2,1,0:T(8,128)(2,1)}, u32[]{:S(2)}, u32[]{:S(2)}) %collective-permute-start.17) | collective-permute-done | bytes 3538976 | tf_op jit(solution)/shard_map/ppermute | solution.py:193
  351.0 22.4 %shard_map.42 = (f32[4,2,64,64]{3,2,1,0:T(8,128)}, f32[4,2,64,64]{3,2,1,0:T(8,128)}) custom-call(s32[108]{0:T(128)} %and_select_fusion.5.tile1, s32[108]{0:T(128)} %select_reduce_fusion.2.tile2, bf16[128,13824]{1,0:T(8,128)(2,1)} %bitcast.282, bf16[128,13824]{1,0:T(8,128)(2,1)} %bitcast.8.refs_1_, bf16[128,13824]{1,0:T(8,128)(2,1)} %bitcast.11.refs_2_, ...), custom_call_target="tpu_custom_call" | custom-call | flops 9059696640 | bytes 17694720 | tf_op jit(solution)/shard_map/pallas_call | solution.py:158
  373.8 1.5 collective-permute-start.39
  375.4 22.4 %shard_map.41 = (f32[4,2,64,64]{3,2,1,0:T(8,128)}, f32[4,2,64,64]{3,2,1,0:T(8,128)}) custom-call(s32[108]{0:T(128)} %and_select_fusion.5.tile1, s32[108]{0:T(128)} %select_reduce_fusion.2.tile2, bf16[128,13824]{1,0:T(8,128)(2,1)} %bitcast.283, bf16[128,13824]{1,0:T(8,128)(2,1)} %bitcast.8.refs_1_, bf16[128,13824]{1,0:T(8,128)(2,1)} %bitcast.11.refs_2_, ...), custom_call_target="tpu_custom_call" | custom-call | flops 9059696640 | bytes 17694720 | tf_op jit(solution)/shard_map/pallas_call | solution.py:158
  398.3 1.1 collective-permute-start.36
  399.4 1.8 collective-permute-start.34
  401.8 1.5 collective-permute-start.31
  403.3 0.9 slice_bitcast_fusion.34
  404.2 4.9 collective-permute-done.27
  409.1 64.3 %collective-permute-start.26 = (f32[4,2,64,64]{3,2,1,0:T(8,128)S(1)}, f32[4,2,64,64]{3,2,1,0:T(8,128)S(1)}, u32[]{:S(2)}, u32[]{:S(2)}) collective-permute-start(f32[4,2,64,64]{3,2,1,0:T(8,128)S(1)} %copy-done.11), channel_id=1, source_target_pairs={{0,10},{1,11},{2,8},{3,9},{4,14},{5,15},{6,12},{7,13},{8,2},{9,3},... | collective-permute-start | bytes 393224 | tf_op jit(solution)/shard_map/ppermute | solution.py:189
  473.6 1.5 collective-permute-start.30
  475.8 0.9 fusion.14
  476.7 4.6 collective-permute-done.30
  481.3 1.6 collective-permute-start.19
  482.9 2.6 collective-permute-start.18
  485.5 0.9 collective-permute-start.13
  486.5 0.9 collective-permute-start.23
  487.4 0.9 fusion.30
  488.3 1.3 collective-permute-start.22
  490.3 0.7 collective-permute-start.20
  491.1 1.7 collective-permute-done.22
  492.8 1.3 collective-permute-done.21
  494.0 11.0 %collective-permute-done.18 = f32[4,2,64,64]{3,2,1,0:T(8,128)S(1)} collective-permute-done((f32[4,2,64,64]{3,2,1,0:T(8,128)S(1)}, f32[4,2,64,64]{3,2,1,0:T(8,128)S(1)}, u32[]{:S(2)}, u32[]{:S(2)}) %collective-permute-start.18) | collective-permute-done | bytes 131104 | tf_op jit(solution)/shard_map/ppermute | solution.py:189
  505.1 4.6 collective-permute-done.13
  509.7 0.9 fusion.46
  511.2 0.8 maximum_bitcast_fusion
  (101 shorter events, 10.6 us)
Async XLA Ops:
  1.0 15.0 %collective-permute-start = (s32[3,13824]{1,0:T(4,128)S(1)}, s32[3,13824]{1,0:T(4,128)S(1)}, u32[]{:S(2)}, u32[]{:S(2)}) collective-permute-start(s32[3,13824]{1,0:T(4,128)S(1)} %bitcast.290), channel_id=1, source_target_pairs={{0,0},{1,2},{6,4},{7,6},{10,8},{11,10},{12,12},{13,14},{18,16},{19... | collective-permute-start | bytes 497672 | tf_op jit(solution)/shard_map/ppermute | solution.py:189
  2.5 8.7 %collective-permute-start.1 = (s32[1,13824]{1,0:T(1,128)S(1)}, s32[1,13824]{1,0:T(1,128)S(1)}, u32[]{:S(2)}, u32[]{:S(2)}) collective-permute-start(s32[1,13824]{1,0:T(1,128)S(1)} %get-tuple-element.88), channel_id=1, source_target_pairs={{16,0},{17,2},{22,4},{23,6},{26,8},{27,10},{28,12},{29,14},{2,16},... | collective-permute-start | bytes 165896 | tf_op jit(solution)/shard_map/ppermute | solution.py:189
  3.8 10.3 %collective-permute-start.2 = (s32[1,13824]{1,0:T(1,128)S(1)}, s32[1,13824]{1,0:T(1,128)S(1)}, u32[]{:S(2)}, u32[]{:S(2)}) collective-permute-start(s32[1,13824]{1,0:T(1,128)S(1)} %get-tuple-element.89), channel_id=1, source_target_pairs={{8,0},{9,2},{14,4},{15,6},{2,8},{3,10},{4,12},{5,14},{26,16},{27,1... | collective-permute-start | bytes 165896 | tf_op jit(solution)/shard_map/ppermute | solution.py:189
  5.1 10.8 %collective-permute-start.3 = (s32[1,13824]{1,0:T(1,128)S(1)}, s32[1,13824]{1,0:T(1,128)S(1)}, u32[]{:S(2)}, u32[]{:S(2)}) collective-permute-start(s32[1,13824]{1,0:T(1,128)S(1)} %get-tuple-element.87), channel_id=1, source_target_pairs={{4,0},{5,2},{2,4},{3,6},{14,8},{15,10},{8,12},{9,14},{22,16},{23,1... | collective-permute-start | bytes 165896 | tf_op jit(solution)/shard_map/ppermute | solution.py:189
  11.3 9.5 %copy-start.4 = (s32[1,13824]{1,0:T(1,128)}, s32[1,13824]{1,0:T(1,128)S(1)}, u32[]{:S(2)}) copy-start(s32[1,13824]{1,0:T(1,128)S(1)} %collective-permute-done.1) | copy-start | bytes 165892
  14.1 6.6 %copy-start.5 = (s32[1,13824]{1,0:T(1,128)}, s32[1,13824]{1,0:T(1,128)S(1)}, u32[]{:S(2)}) copy-start(s32[1,13824]{1,0:T(1,128)S(1)} %collective-permute-done.2) | copy-start | bytes 165892
  16.0 4.8 copy-start.6
  16.0 4.8 copy-start.1
  20.8 80.4 %collective-permute-start.6 = (bf16[2,64,13824]{2,1,0:T(8,128)(2,1)}, bf16[2,64,13824]{2,1,0:T(8,128)(2,1)}, u32[]{:S(2)}, u32[]{:S(2)}) collective-permute-start(bf16[2,64,13824]{2,1,0:T(8,128)(2,1)} %shard_map.40), channel_id=1, source_target_pairs={{0,2},{1,3},{2,0},{3,1},{4,6},{5,7},{6,4},{7,5},{8,10},{9,11},{10,... | collective-permute-start | bytes 10616840 | tf_op jit(solution)/shard_map/ppermute | solution.py:188
  29.7 78.5 %collective-permute-start.5 = (bf16[2,64,13824]{2,1,0:T(8,128)(2,1)}, bf16[2,64,13824]{2,1,0:T(8,128)(2,1)}, u32[]{:S(2)}, u32[]{:S(2)}) collective-permute-start(bf16[2,64,13824]{2,1,0:T(8,128)(2,1)} %shard_map.38), channel_id=1, source_target_pairs={{0,1},{1,0},{2,3},{3,2},{4,5},{5,4},{6,7},{7,6},{8,9},{9,8},{10,11... | collective-permute-start | bytes 10616840 | tf_op jit(solution)/shard_map/ppermute | solution.py:188
  29.8 5.1 copy-start
  29.8 77.6 %copy-start.14 = (f32[1,3]{1,0:T(1,128)S(1)}, f32[1,3]{1,0:T(1,128)}, u32[]{:S(2)}) copy-start(f32[1,3]{1,0:T(1,128)} %param.5) | copy-start | bytes 40
  34.9 79.5 %collective-permute-start.9 = (bf16[2,64,13824]{2,1,0:T(8,128)(2,1)S(1)}, bf16[2,64,13824]{2,1,0:T(8,128)(2,1)}, u32[]{:S(2)}, u32[]{:S(2)}) collective-permute-start(bf16[2,64,13824]{2,1,0:T(8,128)(2,1)S(1)} %copy-done), channel_id=1, source_target_pairs={{0,8},{4,12},{8,0},{12,4},{16,24},{20,28},{24,16},{28,20},{1,9},{5... | collective-permute-start | bytes 10616840 | tf_op jit(solution)/shard_map/ppermute | solution.py:192
  101.2 77.3 %collective-permute-start.7 = (bf16[2,64,13824]{2,1,0:T(8,128)(2,1)}, bf16[2,64,13824]{2,1,0:T(8,128)(2,1)}, u32[]{:S(2)}, u32[]{:S(2)}) collective-permute-start(bf16[2,64,13824]{2,1,0:T(8,128)(2,1)} %shard_map.39), channel_id=1, source_target_pairs={{0,2},{1,3},{2,0},{3,1},{4,6},{5,7},{6,4},{7,5},{8,10},{9,11},{10,... | collective-permute-start | bytes 10616840 | tf_op jit(solution)/shard_map/ppermute | solution.py:188
  104.9 2.5 collective-permute-start.4
  104.9 75.7 %collective-permute-start.11 = (bf16[2,64,13824]{2,1,0:T(8,128)(2,1)S(1)}, bf16[2,64,13824]{2,1,0:T(8,128)(2,1)}, u32[]{:S(2)}, u32[]{:S(2)}) collective-permute-start(bf16[2,64,13824]{2,1,0:T(8,128)(2,1)S(1)} %copy-done), channel_id=1, source_target_pairs={{8,16},{12,20},{16,8},{20,12},{9,17},{13,21},{17,9},{21,13},{10,18... | collective-permute-start | bytes 10616840 | tf_op jit(solution)/shard_map/ppermute | solution.py:193
  107.4 82.8 %collective-permute-start.35 = (bf16[2,64,13824]{2,1,0:T(8,128)(2,1)}, bf16[2,64,13824]{2,1,0:T(8,128)(2,1)}, u32[]{:S(2)}, u32[]{:S(2)}) collective-permute-start(bf16[2,64,13824]{2,1,0:T(8,128)(2,1)} %collective-permute-done.6), channel_id=1, source_target_pairs={{0,4},{4,0},{8,12},{12,8},{16,20},{20,16},{24,28},{28,24},{1,5},{5... | collective-permute-start | bytes 10616840 | tf_op jit(solution)/shard_map/ppermute | solution.py:192
  108.3 84.4 %collective-permute-start.14 = (bf16[2,64,13824]{2,1,0:T(8,128)(2,1)}, bf16[2,64,13824]{2,1,0:T(8,128)(2,1)}, u32[]{:S(2)}, u32[]{:S(2)}) collective-permute-start(bf16[2,64,13824]{2,1,0:T(8,128)(2,1)} %collective-permute-done.6), channel_id=1, source_target_pairs={{0,8},{4,12},{8,0},{12,4},{16,24},{20,28},{24,16},{28,20},{1,9},{5... | collective-permute-start | bytes 10616840 | tf_op jit(solution)/shard_map/ppermute | solution.py:192
  114.4 79.6 %collective-permute-start.16 = (bf16[2,64,13824]{2,1,0:T(8,128)(2,1)}, bf16[2,64,13824]{2,1,0:T(8,128)(2,1)}, u32[]{:S(2)}, u32[]{:S(2)}) collective-permute-start(bf16[2,64,13824]{2,1,0:T(8,128)(2,1)} %collective-permute-done.6), channel_id=1, source_target_pairs={{8,16},{12,20},{16,8},{20,12},{9,17},{13,21},{17,9},{21,13},{10,18... | collective-permute-start | bytes 10616840 | tf_op jit(solution)/shard_map/ppermute | solution.py:193
  178.4 18.0 %collective-permute-start.8 = (bf16[2,64,13824]{2,1,0:T(8,128)(2,1)}, bf16[2,64,13824]{2,1,0:T(8,128)(2,1)}, u32[]{:S(2)}, u32[]{:S(2)}) collective-permute-start(bf16[2,64,13824]{2,1,0:T(8,128)(2,1)} %collective-permute-done.7), channel_id=1, source_target_pairs={{0,1},{1,0},{2,3},{3,2},{4,5},{5,4},{6,7},{7,6},{8,9},{9,8},{10,11... | collective-permute-start | bytes 10616840 | tf_op jit(solution)/shard_map/ppermute | solution.py:188
  180.7 81.9 %collective-permute-start.33 = (bf16[2,64,13824]{2,1,0:T(8,128)(2,1)S(1)}, bf16[2,64,13824]{2,1,0:T(8,128)(2,1)}, u32[]{:S(2)}, u32[]{:S(2)}) collective-permute-start(bf16[2,64,13824]{2,1,0:T(8,128)(2,1)S(1)} %copy-done), channel_id=1, source_target_pairs={{0,4},{4,0},{8,12},{12,8},{16,20},{20,16},{24,28},{28,24},{1,5},{5... | collective-permute-start | bytes 10616840 | tf_op jit(solution)/shard_map/ppermute | solution.py:192
  190.2 183.2 %collective-permute-start.10 = (bf16[2,64,13824]{2,1,0:T(8,128)(2,1)}, bf16[2,64,13824]{2,1,0:T(8,128)(2,1)}, u32[]{:S(2)}, u32[]{:S(2)}) collective-permute-start(bf16[2,64,13824]{2,1,0:T(8,128)(2,1)} %collective-permute-done.9), channel_id=1, source_target_pairs={{8,16},{12,20},{16,8},{20,12},{9,17},{13,21},{17,9},{21,13},{10,18... | collective-permute-start | bytes 10616840 | tf_op jit(solution)/shard_map/ppermute | solution.py:193
  192.7 181.1 %collective-permute-start.12 = (bf16[2,64,13824]{2,1,0:T(8,128)(2,1)}, bf16[2,64,13824]{2,1,0:T(8,128)(2,1)}, u32[]{:S(2)}, u32[]{:S(2)}) collective-permute-start(bf16[2,64,13824]{2,1,0:T(8,128)(2,1)} %collective-permute-done.11), channel_id=1, source_target_pairs={{8,0},{12,4},{16,24},{20,28},{9,1},{13,5},{17,25},{21,29},{10,2},{... | collective-permute-start | bytes 10616840 | tf_op jit(solution)/shard_map/ppermute | solution.py:193
  194.0 134.4 %collective-permute-start.15 = (bf16[2,64,13824]{2,1,0:T(8,128)(2,1)}, bf16[2,64,13824]{2,1,0:T(8,128)(2,1)}, u32[]{:S(2)}, u32[]{:S(2)}) collective-permute-start(bf16[2,64,13824]{2,1,0:T(8,128)(2,1)} %collective-permute-done.14), channel_id=1, source_target_pairs={{8,16},{12,20},{16,8},{20,12},{9,17},{13,21},{17,9},{21,13},{10,18... | collective-permute-start | bytes 10616840 | tf_op jit(solution)/shard_map/ppermute | solution.py:193
  196.4 154.5 %collective-permute-start.17 = (bf16[2,64,13824]{2,1,0:T(8,128)(2,1)}, bf16[2,64,13824]{2,1,0:T(8,128)(2,1)}, u32[]{:S(2)}, u32[]{:S(2)}) collective-permute-start(bf16[2,64,13824]{2,1,0:T(8,128)(2,1)} %collective-permute-done.16), channel_id=1, source_target_pairs={{8,0},{12,4},{16,24},{20,28},{9,1},{13,5},{17,25},{21,29},{10,2},{... | collective-permute-start | bytes 10616840 | tf_op jit(solution)/shard_map/ppermute | solution.py:193
  262.6 135.2 %collective-permute-start.37 = (f32[2,64,64]{2,1,0:T(8,128)}, f32[2,64,64]{2,1,0:T(8,128)S(1)}, u32[]{:S(2)}, u32[]{:S(2)}) collective-permute-start(f32[2,64,64]{2,1,0:T(8,128)} %get-tuple-element.81), channel_id=1, source_target_pairs={{0,2},{1,3},{2,0},{3,1},{4,6},{5,7},{6,4},{7,5},{8,10},{9,11},{10,... | collective-permute-start | bytes 98312 | tf_op jit(solution)/shard_map/ppermute | solution.py:188
  307.1 21.3 %copy-start.8 = (f32[2,64,64]{2,1,0:T(8,128)S(1)}, f32[2,64,64]{2,1,0:T(8,128)}, u32[]{:S(2)}) copy-start(f32[2,64,64]{2,1,0:T(8,128)} %get-tuple-element.82) | copy-start | bytes 98308
  328.4 69.8 %collective-permute-start.42 = (f32[2,64,64]{2,1,0:T(8,128)S(1)}, f32[2,64,64]{2,1,0:T(8,128)S(1)}, u32[]{:S(2)}, u32[]{:S(2)}) collective-permute-start(f32[2,64,64]{2,1,0:T(8,128)S(1)} %copy-done.8), channel_id=1, source_target_pairs={{0,1},{1,0},{2,3},{3,2},{4,5},{5,4},{6,7},{7,6},{8,9},{9,8},{10,11... | collective-permute-start | bytes 98312 | tf_op jit(solution)/shard_map/ppermute | solution.py:188
  351.0 48.4 %collective-permute-start.41 = (f32[2,64,64]{2,1,0:T(8,128)S(1)}, f32[2,64,64]{2,1,0:T(8,128)S(1)}, u32[]{:S(2)}, u32[]{:S(2)}) collective-permute-start(f32[2,64,64]{2,1,0:T(8,128)S(1)} %get-tuple-element.85), channel_id=1, source_target_pairs={{0,3},{1,2},{2,1},{3,0},{4,7},{5,6},{6,5},{7,4},{8,11},{9,10},{10,... | collective-permute-start | bytes 98312 | tf_op jit(solution)/shard_map/ppermute | solution.py:188
  351.0 22.8 %copy-start.7 = (f32[2,64,64]{2,1,0:T(8,128)S(1)}, f32[2,64,64]{2,1,0:T(8,128)}, u32[]{:S(2)}) copy-start(f32[2,64,64]{2,1,0:T(8,128)} %get-tuple-element.83) | copy-start | bytes 98308
  373.4 27.7 %collective-permute-start.40 = (f32[2,64,64]{2,1,0:T(8,128)S(1)}, f32[2,64,64]{2,1,0:T(8,128)S(1)}, u32[]{:S(2)}, u32[]{:S(2)}) collective-permute-start(f32[2,64,64]{2,1,0:T(8,128)S(1)} %get-tuple-element.86), channel_id=1, source_target_pairs={{0,2},{1,3},{2,0},{3,1},{4,6},{5,7},{6,4},{7,5},{8,10},{9,11},{10,... | collective-permute-start | bytes 98312 | tf_op jit(solution)/shard_map/ppermute | solution.py:188
  373.8 28.0 %collective-permute-start.39 = (f32[2,64,64]{2,1,0:T(8,128)S(1)}, f32[2,64,64]{2,1,0:T(8,128)S(1)}, u32[]{:S(2)}, u32[]{:S(2)}) collective-permute-start(f32[2,64,64]{2,1,0:T(8,128)S(1)} %copy-done.7), channel_id=1, source_target_pairs={{0,3},{1,2},{2,1},{3,0},{4,7},{5,6},{6,5},{7,4},{8,11},{9,10},{10,... | collective-permute-start | bytes 98312 | tf_op jit(solution)/shard_map/ppermute | solution.py:188
  375.3 22.5 %copy-start.3 = (f32[4,2,64,64]{3,2,1,0:T(8,128)S(1)}, f32[4,2,64,64]{3,2,1,0:T(8,128)}, u32[]{:S(2)}) copy-start(f32[4,2,64,64]{3,2,1,0:T(8,128)} %get-tuple-element.37) | copy-start | bytes 393220
  375.3 22.9 %copy-start.2 = (f32[4,2,64,64]{3,2,1,0:T(8,128)S(1)}, f32[4,2,64,64]{3,2,1,0:T(8,128)}, u32[]{:S(2)}) copy-start(f32[4,2,64,64]{3,2,1,0:T(8,128)} %get-tuple-element.35) | copy-start | bytes 393220
  375.3 22.9 %copy-start.12 = (f32[4,2,64,64]{3,2,1,0:T(8,128)S(1)}, f32[4,2,64,64]{3,2,1,0:T(8,128)}, u32[]{:S(2)}) copy-start(f32[4,2,64,64]{3,2,1,0:T(8,128)} %get-tuple-element.43) | copy-start | bytes 393220
  375.3 24.1 %copy-start.13 = (f32[4,2,64,64]{3,2,1,0:T(8,128)S(1)}, f32[4,2,64,64]{3,2,1,0:T(8,128)}, u32[]{:S(2)}) copy-start(f32[4,2,64,64]{3,2,1,0:T(8,128)} %get-tuple-element.41) | copy-start | bytes 393220
  375.3 33.8 %copy-start.11 = (f32[4,2,64,64]{3,2,1,0:T(8,128)S(1)}, f32[4,2,64,64]{3,2,1,0:T(8,128)}, u32[]{:S(2)}) copy-start(f32[4,2,64,64]{3,2,1,0:T(8,128)} %get-tuple-element.38) | copy-start | bytes 393220
  375.3 98.0 %copy-start.10 = (f32[4,2,64,64]{3,2,1,0:T(8,128)S(1)}, f32[4,2,64,64]{3,2,1,0:T(8,128)}, u32[]{:S(2)}) copy-start(f32[4,2,64,64]{3,2,1,0:T(8,128)} %get-tuple-element.36) | copy-start | bytes 393220
  375.4 107.5 %copy-start.9 = (f32[4,2,64,64]{3,2,1,0:T(8,128)S(1)}, f32[4,2,64,64]{3,2,1,0:T(8,128)}, u32[]{:S(2)}) copy-start(f32[4,2,64,64]{3,2,1,0:T(8,128)} %get-tuple-element.34) | copy-start | bytes 393220
  397.8 4.0 collective-permute-start.38
  398.3 76.8 %collective-permute-start.36 = (f32[4,2,64,64]{3,2,1,0:T(8,128)S(1)}, f32[4,2,64,64]{3,2,1,0:T(8,128)S(1)}, u32[]{:S(2)}, u32[]{:S(2)}) collective-permute-start(f32[4,2,64,64]{3,2,1,0:T(8,128)S(1)} %copy-done.12), channel_id=1, source_target_pairs={{0,6},{1,7},{2,4},{3,5},{4,2},{5,3},{6,0},{7,1},{8,14},{9,15},{10,... | collective-permute-start | bytes 393224 | tf_op jit(solution)/shard_map/ppermute | solution.py:189
  399.4 75.7 %collective-permute-start.34 = (f32[4,2,64,64]{3,2,1,0:T(8,128)S(1)}, f32[4,2,64,64]{3,2,1,0:T(8,128)S(1)}, u32[]{:S(2)}, u32[]{:S(2)}) collective-permute-start(f32[4,2,64,64]{3,2,1,0:T(8,128)S(1)} %copy-done.13), channel_id=1, source_target_pairs={{0,4},{1,5},{2,6},{3,7},{4,0},{5,1},{6,2},{7,3},{8,12},{9,13},{10,... | collective-permute-start | bytes 393224 | tf_op jit(solution)/shard_map/ppermute | solution.py:189
  401.2 8.0 %collective-permute-start.27 = (f32[2,64,64]{2,1,0:T(8,128)S(1)}, f32[2,64,64]{2,1,0:T(8,128)S(1)}, u32[]{:S(2)}, u32[]{:S(2)}) collective-permute-start(f32[2,64,64]{2,1,0:T(8,128)S(1)} %get-tuple-element.75), channel_id=1, source_target_pairs={{0,2},{1,3},{2,0},{3,1},{4,6},{5,7},{6,4},{7,5},{8,10},{9,11},{10,... | collective-permute-start | bytes 98312 | tf_op jit(solution)/shard_map/ppermute | solution.py:188
  401.8 71.6 %collective-permute-start.32 = (f32[2,64,64]{2,1,0:T(8,128)S(1)}, f32[2,64,64]{2,1,0:T(8,128)S(1)}, u32[]{:S(2)}, u32[]{:S(2)}) collective-permute-start(f32[2,64,64]{2,1,0:T(8,128)S(1)} %get-tuple-element.76), channel_id=1, source_target_pairs={{0,1},{1,0},{2,3},{3,2},{4,5},{5,4},{6,7},{7,6},{8,9},{9,8},{10,11... | collective-permute-start | bytes 98312 | tf_op jit(solution)/shard_map/ppermute | solution.py:188
  401.8 71.8 %collective-permute-start.31 = (f32[2,64,64]{2,1,0:T(8,128)S(1)}, f32[2,64,64]{2,1,0:T(8,128)S(1)}, u32[]{:S(2)}, u32[]{:S(2)}) collective-permute-start(f32[2,64,64]{2,1,0:T(8,128)S(1)} %get-tuple-element.79), channel_id=1, source_target_pairs={{0,3},{1,2},{2,1},{3,0},{4,7},{5,6},{6,5},{7,4},{8,11},{9,10},{10,... | collective-permute-start | bytes 98312 | tf_op jit(solution)/shard_map/ppermute | solution.py:188
  409.1 77.3 %collective-permute-start.26 = (f32[4,2,64,64]{3,2,1,0:T(8,128)S(1)}, f32[4,2,64,64]{3,2,1,0:T(8,128)S(1)}, u32[]{:S(2)}, u32[]{:S(2)}) collective-permute-start(f32[4,2,64,64]{3,2,1,0:T(8,128)S(1)} %copy-done.11), channel_id=1, source_target_pairs={{0,10},{1,11},{2,8},{3,9},{4,14},{5,15},{6,12},{7,13},{8,2},{9,3},... | collective-permute-start | bytes 393224 | tf_op jit(solution)/shard_map/ppermute | solution.py:189
  473.4 13.1 %collective-permute-start.25 = (f32[4,2,64,64]{3,2,1,0:T(8,128)S(1)}, f32[4,2,64,64]{3,2,1,0:T(8,128)S(1)}, u32[]{:S(2)}, u32[]{:S(2)}) collective-permute-start(f32[4,2,64,64]{3,2,1,0:T(8,128)S(1)} %copy-done.10), channel_id=1, source_target_pairs={{0,8},{1,9},{2,10},{3,11},{4,12},{5,13},{6,14},{7,15},{8,0},{9,1},... | collective-permute-start | bytes 393224 | tf_op jit(solution)/shard_map/ppermute | solution.py:189
  473.6 7.7 %collective-permute-start.30 = (f32[2,64,64]{2,1,0:T(8,128)S(1)}, f32[2,64,64]{2,1,0:T(8,128)S(1)}, u32[]{:S(2)}, u32[]{:S(2)}) collective-permute-start(f32[2,64,64]{2,1,0:T(8,128)S(1)} %get-tuple-element.80), channel_id=1, source_target_pairs={{0,2},{1,3},{2,0},{3,1},{4,6},{5,7},{6,4},{7,5},{8,10},{9,11},{10,... | collective-permute-start | bytes 98312 | tf_op jit(solution)/shard_map/ppermute | solution.py:188
  475.1 7.8 %collective-permute-start.29 = (f32[2,64,64]{2,1,0:T(8,128)S(1)}, f32[2,64,64]{2,1,0:T(8,128)S(1)}, u32[]{:S(2)}, u32[]{:S(2)}) collective-permute-start(f32[2,64,64]{2,1,0:T(8,128)S(1)} %get-tuple-element.77), channel_id=1, source_target_pairs={{0,3},{1,2},{2,1},{3,0},{4,7},{5,6},{6,5},{7,4},{8,11},{9,10},{10,... | collective-permute-start | bytes 98312 | tf_op jit(solution)/shard_map/ppermute | solution.py:188
  475.1 10.4 %collective-permute-start.28 = (f32[2,64,64]{2,1,0:T(8,128)S(1)}, f32[2,64,64]{2,1,0:T(8,128)S(1)}, u32[]{:S(2)}, u32[]{:S(2)}) collective-permute-start(f32[2,64,64]{2,1,0:T(8,128)S(1)} %get-tuple-element.78), channel_id=1, source_target_pairs={{0,1},{1,0},{2,3},{3,2},{4,5},{5,4},{6,7},{7,6},{8,9},{9,8},{10,11... | collective-permute-start | bytes 98312 | tf_op jit(solution)/shard_map/ppermute | solution.py:188
  481.3 7.1 %collective-permute-start.19 = (f32[2,64,64]{2,1,0:T(8,128)S(1)}, f32[2,64,64]{2,1,0:T(8,128)S(1)}, u32[]{:S(2)}, u32[]{:S(2)}) collective-permute-start(f32[2,64,64]{2,1,0:T(8,128)S(1)} %get-tuple-element.69), channel_id=1, source_target_pairs={{0,2},{1,3},{2,0},{3,1},{4,6},{5,7},{6,4},{7,5},{8,10},{9,11},{10,... | collective-permute-start | bytes 98312 | tf_op jit(solution)/shard_map/ppermute | solution.py:188
  482.9 22.2 %collective-permute-start.18 = (f32[4,2,64,64]{3,2,1,0:T(8,128)S(1)}, f32[4,2,64,64]{3,2,1,0:T(8,128)S(1)}, u32[]{:S(2)}, u32[]{:S(2)}) collective-permute-start(f32[4,2,64,64]{3,2,1,0:T(8,128)S(1)} %copy-done.9), channel_id=1, source_target_pairs={{0,18},{1,19},{2,16},{3,17},{4,22},{5,23},{6,20},{7,21},{8,26},{9,... | collective-permute-start | bytes 393224 | tf_op jit(solution)/shard_map/ppermute | solution.py:189
  485.5 24.2 %collective-permute-start.13 = (f32[4,2,64,64]{3,2,1,0:T(8,128)}, f32[4,2,64,64]{3,2,1,0:T(8,128)S(1)}, u32[]{:S(2)}, u32[]{:S(2)}) collective-permute-start(f32[4,2,64,64]{3,2,1,0:T(8,128)} %get-tuple-element.32), channel_id=1, source_target_pairs={{0,16},{1,17},{2,18},{3,19},{4,20},{5,21},{6,22},{7,23},{8,24},{9,... | collective-permute-start | bytes 393224 | tf_op jit(solution)/shard_map/ppermute | solution.py:189
  486.5 3.2 collective-permute-start.24
  486.5 3.8 collective-permute-start.23
  488.3 4.4 collective-permute-start.22
  489.6 4.4 collective-permute-start.21
  490.3 3.7 collective-permute-start.20
where the time goes:
time: 515 us; the launch traced here: 512 us
  waiting for transfers between devices  228 us (44%)
  Pallas kernels  149 us (29%)
  starting transfers between devices  114 us (22%)
  other arithmetic  13.1 us (3%)
  local copies, waits for them, and re-layouts  7.87 us (2%)
    ppermute x23, waiting for transfers between devices, paired_points(): lax.ppermute(value, 'ga', [(s, s ^ mask) for s in range(group)])  139 us
    pallas_call x6, Pallas kernels, pair_products(): pl.pallas_call(functools.partial(pair_body, unroll), grid_spec=grid_spec,...  130 us
    ppermute x10, starting transfers between devices, paired_points(): both = lambda value, pairs: lax.ppermute(value, ('ka', 'ga'), pairs)  75.5 us
    ppermute x4, waiting for transfers between devices, paired_points(): lax.ppermute(value, 'ka', [(s, s ^ flips[b]) for s in range(points)])  45.7 us
    ppermute x6, waiting for transfers between devices, paired_points(): along = lambda value, pairs: lax.ppermute(value, 'ka', pairs)  22.5 us
    ppermute x10, waiting for transfers between devices, paired_points(): both = lambda value, pairs: lax.ppermute(value, ('ka', 'ga'), pairs)  20.4 us
    pallas_call x4, Pallas kernels, block_of(): pl.pallas_call(copy_body, grid_spec=grid_spec, out_shape=jax.ShapeDtypeSt...  19.3 us
    ppermute x23, starting transfers between devices, paired_points(): lax.ppermute(value, 'ga', [(s, s ^ mask) for s in range(group)])  17.7 us
  transfers between devices with their start and end apart: 43, of which 15 were waited for; matrix products, arithmetic and copies ran while one was open for 3% of the time, Pallas kernels for 28%

commit v1 on v0

--- a/solution.py
+++ b/solution.py
@@ -9,7 +9,7 @@
 
 
 LANES = 128
-UNROLL = 6
+UNROLL = 27
 F32 = jnp.float32
 NT = (((1,), (1,)), ((), ()))
 
@@ -193,21 +193,18 @@
     along = lambda value, pairs: lax.ppermute(value, "ka", pairs)
 
     maps = shift_map[0]
-    arrived = [
-        both(
-            value,
-            [
-                ((p ^ flip) * group + parity_of(p) * half + y, p * group + 2 * y)
-                for p in range(points)
-                for y in range(half)
-            ],
-        )
-        for value, flip in [(maps, 0)] + [(maps[b : b + 1], flips[b]) for b in range(3)]
-    ]
+    arrived = []
+    for value, flip in [(maps, 0)] + [(maps[b : b + 1], flips[b]) for b in range(3)]:
+        pairs = [
+            ((p ^ flip) * group + parity_of(p) * half + y, p * group + 2 * y)
+            for p in range(points)
+            for y in range(half)
+        ]
+        arrived.append(both(value, pairs))
     out_own = block_of(raw, theirs, width)
-    out_own, *arrived = lax.optimization_barrier((out_own, *arrived))
     arrived = jnp.concatenate(arrived, axis=0)
-    arrived = jnp.where(j % 2 == 0, arrived, mates(arrived, 1)) - mine * width
+    swapped_maps = mates(arrived, 1)
+    arrived = jnp.where(j % 2 == 0, arrived, swapped_maps) - mine * width
 
     first1 = hop(out_own, 1)
     parked0 = along(out_own, middle)

time: 515 us -> 565 us (1.097)
  starting transfers between devices: 114 us -> 170 us
  Pallas kernels: 149 us -> 101 us
  waiting for transfers between devices: 228 us -> 272 us
    ppermute x4, waiting for transfers between devices: 45.7 us -> 117 us  [paired_points(): lax.ppermute(value, 'ka', [(s, s ^ flips[b]) for s in range(points)])]
    ppermute x23, starting transfers between devices: 17.7 us -> 76.7 us  [paired_points(): lax.ppermute(value, 'ga', [(s, s ^ mask) for s in range(group)])]
    ppermute x23, waiting for transfers between devices: 139 us -> 80.7 us  [paired_points(): lax.ppermute(value, 'ga', [(s, s ^ mask) for s in range(group)])]
    pallas_call x6, Pallas kernels: 130 us -> 82.3 us  [pair_products(): pl.pallas_call(functools.partial(pair_body, unroll), grid_spec=grid_spec,...]
    ppermute x6, waiting for transfers between devices: 22.5 us -> 44.8 us  [paired_points(): along = lambda value, pairs: lax.ppermute(value, 'ka', pairs)]
    ppermute x10, waiting for transfers between devices: 20.4 us -> 30 us  [paired_points(): both = lambda value, pairs: lax.ppermute(value, ('ka', 'ga'), pairs)]
  transfers between devices with their start and end apart: 43 -> 43, of which waited for: 15 -> 15; matrix products, arithmetic and copies ran while one was open for 3% -> 3% of each run, Pallas kernels for 28% -> 16%
where the time goes in v1:
time: 565 us; the launch traced here: 564 us
  waiting for transfers between devices  272 us (48%)
  starting transfers between devices  170 us (30%)
  Pallas kernels  101 us (18%)
  other arithmetic  12 us (2%)
  local copies, waits for them, and re-layouts  7.87 us (1%)
    ppermute x4, waiting for transfers between devices, paired_points(): lax.ppermute(value, 'ka', [(s, s ^ flips[b]) for s in range(points)])  117 us
    pallas_call x6, Pallas kernels, pair_products(): pl.pallas_call(functools.partial(pair_body, unroll), grid_spec=grid_spec,...  82.3 us
    ppermute x23, waiting for transfers between devices, paired_points(): lax.ppermute(value, 'ga', [(s, s ^ mask) for s in range(group)])  80.7 us
    ppermute x23, starting transfers between devices, paired_points(): lax.ppermute(value, 'ga', [(s, s ^ mask) for s in range(group)])  76.7 us
    ppermute x10, starting transfers between devices, paired_points(): both = lambda value, pairs: lax.ppermute(value, ('ka', 'ga'), pairs)  73.6 us
    ppermute x6, waiting for transfers between devices, paired_points(): along = lambda value, pairs: lax.ppermute(value, 'ka', pairs)  44.8 us
    ppermute x10, waiting for transfers between devices, paired_points(): both = lambda value, pairs: lax.ppermute(value, ('ka', 'ga'), pairs)  30 us
    pallas_call x4, Pallas kernels, block_of(): pl.pallas_call(copy_body, grid_spec=grid_spec, out_shape=jax.ShapeDtypeSt...  19.1 us
  transfers between devices with their start and end apart: 43, of which 15 were waited for; matrix products, arithmetic and copies ran while one was open for 3% of the time, Pallas kernels for 16%

profile of v1, /device:TPU:0, one launch (start us, length us, event | category | flops | bytes accessed | tf_op | source)
XLA Modules:
  0.0 563.8 jit_solution(11995474557645337850)
XLA Ops:
  0.0 4.7 shard_map.39
  4.7 5.1 shard_map.40
  9.7 3.0 collective-permute-start.6
  12.7 1.6 collective-permute-start.9
  14.3 4.7 shard_map.37
  19.0 4.7 shard_map.38
  23.7 65.9 %collective-permute-done.6 = bf16[2,64,13824]{2,1,0:T(8,128)(2,1)} collective-permute-done((bf16[2,64,13824]{2,1,0:T(8,128)(2,1)}, bf16[2,64,13824]{2,1,0:T(8,128)(2,1)}, u32[]{:S(2)}, u32[]{:S(2)}) %collective-permute-start.6) | collective-permute-done | bytes 3538976 | tf_op jit(solution)/shard_map/ppermute | solution.py:188
  89.6 1.7 collective-permute-start.7
  91.3 0.9 slice_bitcast_fusion.38
  92.2 1.3 collective-permute-start.3
  93.5 1.0 copy.6
  95.2 3.1 collective-permute-done.3
  98.3 1.3 collective-permute-start.2
  99.5 5.3 collective-permute-done.2
  104.9 1.3 collective-permute-start.1
  106.2 6.7 %collective-permute-done.1 = s32[1,13824]{1,0:T(1,128)S(1)} collective-permute-done((s32[1,13824]{1,0:T(1,128)S(1)}, s32[1,13824]{1,0:T(1,128)S(1)}, u32[]{:S(2)}, u32[]{:S(2)}) %collective-permute-start.1) | collective-permute-done | bytes 55328 | tf_op jit(solution)/shard_map/ppermute | solution.py:189
  112.9 1.0 pad_add_fusion
  113.9 57.8 %collective-permute-start.4 = (s32[6,13824]{1,0:T(8,128)}, s32[6,13824]{1,0:T(8,128)}, u32[]{:S(2)}, u32[]{:S(2)}) collective-permute-start(s32[6,13824]{1,0:T(8,128)} %pad_add_fusion), channel_id=1, source_target_pairs={{0,1},{1,0},{2,3},{3,2},{4,5},{5,4},{6,7},{7,6},{8,9},{9,8},{10,11... | collective-permute-start | bytes 995336 | tf_op jit(solution)/shard_map/ppermute | solution.py:188
  171.7 2.5 collective-permute-start.11
  174.2 2.4 collective-permute-start.35
  176.7 1.8 collective-permute-start.14
  178.4 2.4 collective-permute-start.16
  180.9 1.2 select_subtract_fusion
  182.1 0.9 slice_reduce_fusion.10
  183.1 1.5 collective-permute-start.33
  191.0 63.4 %collective-permute-done.35 = bf16[2,64,13824]{2,1,0:T(8,128)(2,1)} collective-permute-done((bf16[2,64,13824]{2,1,0:T(8,128)(2,1)}, bf16[2,64,13824]{2,1,0:T(8,128)(2,1)}, u32[]{:S(2)}, u32[]{:S(2)}) %collective-permute-start.35) | collective-permute-done | bytes 3538976 | tf_op jit(solution)/shard_map/ppermute | solution.py:192
  254.4 2.5 collective-permute-start.10
  256.8 1.3 collective-permute-start.12
  258.1 2.4 collective-permute-start.15
  260.6 1.5 collective-permute-start.17
  262.0 13.2 %shard_map.46 = (f32[4,2,64,64]{3,2,1,0:T(8,128)}, f32[4,2,64,64]{3,2,1,0:T(8,128)}) custom-call(s32[108]{0:T(128)} %get-tuple-element.83.tile1, s32[108]{0:T(128)} %select_reduce_fusion.tile2, bf16[128,13824]{1,0:T(8,128)(2,1)} %bitcast.278, bf16[128,13824]{1,0:T(8,128)(2,1)} %bitcast.7.refs_1_, bf16[128,13824]{1,0:T(8,128)(2,1)} %bitcast.11.refs_2_, ...), custom_call_target="tpu_custom_call" | custom-call | flops 9059696640 | bytes 17694720 | tf_op jit(solution)/shard_map/pallas_call | solution.py:158
  275.3 1.6 slice_bitcast_fusion.23
  276.8 53.2 %collective-permute-done.33 = bf16[2,64,13824]{2,1,0:T(8,128)(2,1)} collective-permute-done((bf16[2,64,13824]{2,1,0:T(8,128)(2,1)S(1)}, bf16[2,64,13824]{2,1,0:T(8,128)(2,1)}, u32[]{:S(2)}, u32[]{:S(2)}) %collective-permute-start.33) | collective-permute-done | bytes 3538976 | tf_op jit(solution)/shard_map/ppermute | solution.py:192
  330.0 1.8 collective-permute-start.37
  331.8 13.2 %shard_map.45 = (f32[4,2,64,64]{3,2,1,0:T(8,128)}, f32[4,2,64,64]{3,2,1,0:T(8,128)}) custom-call(s32[108]{0:T(128)} %get-tuple-element.83.tile1, s32[108]{0:T(128)} %select_reduce_fusion.tile2, bf16[128,13824]{1,0:T(8,128)(2,1)} %bitcast.279, bf16[128,13824]{1,0:T(8,128)(2,1)} %bitcast.7.refs_1_, bf16[128,13824]{1,0:T(8,128)(2,1)} %bitcast.11.refs_2_, ...), custom_call_target="tpu_custom_call" | custom-call | flops 9059696640 | bytes 17694720 | tf_op jit(solution)/shard_map/pallas_call | solution.py:158
  345.0 0.9 slice_bitcast_fusion.22
  345.9 13.3 %shard_map.44 = (f32[4,2,64,64]{3,2,1,0:T(8,128)}, f32[4,2,64,64]{3,2,1,0:T(8,128)}) custom-call(s32[108]{0:T(128)} %get-tuple-element.85.tile1, s32[108]{0:T(128)} %select_reduce_fusion.1.tile2, bf16[128,13824]{1,0:T(8,128)(2,1)} %bitcast.280, bf16[128,13824]{1,0:T(8,128)(2,1)} %bitcast.7.refs_1_, bf16[128,13824]{1,0:T(8,128)(2,1)} %bitcast.11.refs_2_, ...), custom_call_target="tpu_custom_call" | custom-call | flops 9059696640 | bytes 17694720 | tf_op jit(solution)/shard_map/pallas_call | solution.py:158
  359.2 0.9 slice_bitcast_fusion.29
  360.1 13.4 %shard_map.43 = (f32[4,2,64,64]{3,2,1,0:T(8,128)}, f32[4,2,64,64]{3,2,1,0:T(8,128)}) custom-call(s32[108]{0:T(128)} %get-tuple-element.85.tile1, s32[108]{0:T(128)} %select_reduce_fusion.1.tile2, bf16[128,13824]{1,0:T(8,128)(2,1)} %bitcast.281, bf16[128,13824]{1,0:T(8,128)(2,1)} %bitcast.7.refs_1_, bf16[128,13824]{1,0:T(8,128)(2,1)} %bitcast.11.refs_2_, ...), custom_call_target="tpu_custom_call" | custom-call | flops 9059696640 | bytes 17694720 | tf_op jit(solution)/shard_map/pallas_call | solution.py:158
  373.6 44.8 %collective-permute-done.17 = bf16[2,64,13824]{2,1,0:T(8,128)(2,1)} collective-permute-done((bf16[2,64,13824]{2,1,0:T(8,128)(2,1)}, bf16[2,64,13824]{2,1,0:T(8,128)(2,1)}, u32[]{:S(2)}, u32[]{:S(2)}) %collective-permute-start.17) | collective-permute-done | bytes 3538976 | tf_op jit(solution)/shard_map/ppermute | solution.py:193
  418.8 14.4 %shard_map.42 = (f32[4,2,64,64]{3,2,1,0:T(8,128)}, f32[4,2,64,64]{3,2,1,0:T(8,128)}) custom-call(s32[108]{0:T(128)} %and_select_fusion.5.tile1, s32[108]{0:T(128)} %select_reduce_fusion.2.tile2, bf16[128,13824]{1,0:T(8,128)(2,1)} %bitcast.282, bf16[128,13824]{1,0:T(8,128)(2,1)} %bitcast.7.refs_1_, bf16[128,13824]{1,0:T(8,128)(2,1)} %bitcast.11.refs_2_, ...), custom_call_target="tpu_custom_call" | custom-call | flops 9059696640 | bytes 17694720 | tf_op jit(solution)/shard_map/pallas_call | solution.py:158
  433.2 2.5 collective-permute-start.40
  435.7 1.4 collective-permute-start.39
  437.2 14.7 %shard_map.41 = (f32[4,2,64,64]{3,2,1,0:T(8,128)}, f32[4,2,64,64]{3,2,1,0:T(8,128)}) custom-call(s32[108]{0:T(128)} %and_select_fusion.5.tile1, s32[108]{0:T(128)} %select_reduce_fusion.2.tile2, bf16[128,13824]{1,0:T(8,128)(2,1)} %bitcast.283, bf16[128,13824]{1,0:T(8,128)(2,1)} %bitcast.7.refs_1_, bf16[128,13824]{1,0:T(8,128)(2,1)} %bitcast.11.refs_2_, ...), custom_call_target="tpu_custom_call" | custom-call | flops 9059696640 | bytes 17694720 | tf_op jit(solution)/shard_map/pallas_call | solution.py:158
  452.6 1.7 collective-permute-start.34
  454.3 1.3 collective-permute-start.27
  455.6 0.8 collective-permute-start.31
  456.4 0.9 slice_bitcast_fusion.34
  457.3 5.8 %collective-permute-done.27 = f32[2,64,64]{2,1,0:T(8,128)S(1)} collective-permute-done((f32[2,64,64]{2,1,0:T(8,128)S(1)}, f32[2,64,64]{2,1,0:T(8,128)S(1)}, u32[]{:S(2)}, u32[]{:S(2)}) %collective-permute-start.27) | collective-permute-done | bytes 32800 | tf_op jit(solution)/shard_map/ppermute | solution.py:188
  463.2 63.2 %collective-permute-start.26 = (f32[4,2,64,64]{3,2,1,0:T(8,128)S(1)}, f32[4,2,64,64]{3,2,1,0:T(8,128)S(1)}, u32[]{:S(2)}, u32[]{:S(2)}) collective-permute-start(f32[4,2,64,64]{3,2,1,0:T(8,128)S(1)} %copy-done.11), channel_id=1, source_target_pairs={{0,10},{1,11},{2,8},{3,9},{4,14},{5,15},{6,12},{7,13},{8,2},{9,3},... | collective-permute-start | bytes 393224 | tf_op jit(solution)/shard_map/ppermute | solution.py:189
  527.5 1.1 collective-permute-start.28
  528.6 0.9 fusion.14
  529.6 4.7 collective-permute-done.30
  534.7 0.8 collective-permute-done.29
  535.5 3.7 collective-permute-start.18
  539.2 0.9 collective-permute-start.23
  540.1 0.9 fusion.30
  541.1 1.3 collective-permute-start.22
  543.8 1.7 collective-permute-done.22
  545.6 1.2 collective-permute-done.21
  546.8 10.9 %collective-permute-done.18 = f32[4,2,64,64]{3,2,1,0:T(8,128)S(1)} collective-permute-done((f32[4,2,64,64]{3,2,1,0:T(8,128)S(1)}, f32[4,2,64,64]{3,2,1,0:T(8,128)S(1)}, u32[]{:S(2)}, u32[]{:S(2)}) %collective-permute-start.18) | collective-permute-done | bytes 131104 | tf_op jit(solution)/shard_map/ppermute | solution.py:189
  557.7 3.9 collective-permute-done.13
  561.6 0.9 fusion.46
  563.0 0.8 maximum_bitcast_fusion
  (101 shorter events, 12.0 us)
Async XLA Ops:
  4.7 8.1 %copy-start = (bf16[2,64,13824]{2,1,0:T(8,128)(2,1)S(1)}, bf16[2,64,13824]{2,1,0:T(8,128)(2,1)}, u32[]{:S(2)}) copy-start(bf16[2,64,13824]{2,1,0:T(8,128)(2,1)} %shard_map.39) | copy-start | bytes 10616836
  9.7 79.8 %collective-permute-start.6 = (bf16[2,64,13824]{2,1,0:T(8,128)(2,1)}, bf16[2,64,13824]{2,1,0:T(8,128)(2,1)}, u32[]{:S(2)}, u32[]{:S(2)}) collective-permute-start(bf16[2,64,13824]{2,1,0:T(8,128)(2,1)} %shard_map.40), channel_id=1, source_target_pairs={{0,2},{1,3},{2,0},{3,1},{4,6},{5,7},{6,4},{7,5},{8,10},{9,11},{10,... | collective-permute-start | bytes 10616840 | tf_op jit(solution)/shard_map/ppermute | solution.py:188
  12.7 165.7 %collective-permute-start.9 = (bf16[2,64,13824]{2,1,0:T(8,128)(2,1)S(1)}, bf16[2,64,13824]{2,1,0:T(8,128)(2,1)}, u32[]{:S(2)}, u32[]{:S(2)}) collective-permute-start(bf16[2,64,13824]{2,1,0:T(8,128)(2,1)S(1)} %copy-done), channel_id=1, source_target_pairs={{0,8},{4,12},{8,0},{12,4},{16,24},{20,28},{24,16},{28,20},{1,9},{5... | collective-permute-start | bytes 10616840 | tf_op jit(solution)/shard_map/ppermute | solution.py:192
  19.0 157.7 %collective-permute-start.5 = (bf16[2,64,13824]{2,1,0:T(8,128)(2,1)}, bf16[2,64,13824]{2,1,0:T(8,128)(2,1)}, u32[]{:S(2)}, u32[]{:S(2)}) collective-permute-start(bf16[2,64,13824]{2,1,0:T(8,128)(2,1)} %shard_map.37), channel_id=1, source_target_pairs={{0,1},{1,0},{2,3},{3,2},{4,5},{5,4},{6,7},{7,6},{8,9},{9,8},{10,11... | collective-permute-start | bytes 10616840 | tf_op jit(solution)/shard_map/ppermute | solution.py:188
  19.0 155.2 %copy-start.14 = (f32[1,3]{1,0:T(1,128)S(1)}, f32[1,3]{1,0:T(1,128)}, u32[]{:S(2)}) copy-start(f32[1,3]{1,0:T(1,128)} %param.5) | copy-start | bytes 40
  89.6 91.3 %collective-permute-start.7 = (bf16[2,64,13824]{2,1,0:T(8,128)(2,1)}, bf16[2,64,13824]{2,1,0:T(8,128)(2,1)}, u32[]{:S(2)}, u32[]{:S(2)}) collective-permute-start(bf16[2,64,13824]{2,1,0:T(8,128)(2,1)} %shard_map.38), channel_id=1, source_target_pairs={{0,2},{1,3},{2,0},{3,1},{4,6},{5,7},{6,4},{7,5},{8,10},{9,11},{10,... | collective-permute-start | bytes 10616840 | tf_op jit(solution)/shard_map/ppermute | solution.py:188
  92.2 6.0 %collective-permute-start.3 = (s32[1,13824]{1,0:T(1,128)S(1)}, s32[1,13824]{1,0:T(1,128)S(1)}, u32[]{:S(2)}, u32[]{:S(2)}) collective-permute-start(s32[1,13824]{1,0:T(1,128)S(1)} %get-tuple-element.78), channel_id=1, source_target_pairs={{4,0},{5,2},{2,4},{3,6},{14,8},{15,10},{8,12},{9,14},{22,16},{23,1... | collective-permute-start | bytes 165896 | tf_op jit(solution)/shard_map/ppermute | solution.py:189
  94.5 18.4 %collective-permute-start = (s32[3,13824]{1,0:T(4,128)S(1)}, s32[3,13824]{1,0:T(4,128)S(1)}, u32[]{:S(2)}, u32[]{:S(2)}) collective-permute-start(s32[3,13824]{1,0:T(4,128)S(1)} %bitcast.290), channel_id=1, source_target_pairs={{0,0},{1,2},{6,4},{7,6},{10,8},{11,10},{12,12},{13,14},{18,16},{19... | collective-permute-start | bytes 497672 | tf_op jit(solution)/shard_map/ppermute | solution.py:189
  98.2 73.5 %copy-start.4 = (s32[1,13824]{1,0:T(1,128)}, s32[1,13824]{1,0:T(1,128)S(1)}, u32[]{:S(2)}) copy-start(s32[1,13824]{1,0:T(1,128)S(1)} %collective-permute-done.3) | copy-start | bytes 165892
  98.3 6.6 %collective-permute-start.2 = (s32[1,13824]{1,0:T(1,128)S(1)}, s32[1,13824]{1,0:T(1,128)S(1)}, u32[]{:S(2)}, u32[]{:S(2)}) collective-permute-start(s32[1,13824]{1,0:T(1,128)S(1)} %get-tuple-element.79), channel_id=1, source_target_pairs={{8,0},{9,2},{14,4},{15,6},{2,8},{3,10},{4,12},{5,14},{26,16},{27,1... | collective-permute-start | bytes 165896 | tf_op jit(solution)/shard_map/ppermute | solution.py:189
  104.9 69.3 %copy-start.5 = (s32[1,13824]{1,0:T(1,128)}, s32[1,13824]{1,0:T(1,128)S(1)}, u32[]{:S(2)}) copy-start(s32[1,13824]{1,0:T(1,128)S(1)} %collective-permute-done.2) | copy-start | bytes 165892
  104.9 8.0 %collective-permute-start.1 = (s32[1,13824]{1,0:T(1,128)S(1)}, s32[1,13824]{1,0:T(1,128)S(1)}, u32[]{:S(2)}, u32[]{:S(2)}) collective-permute-start(s32[1,13824]{1,0:T(1,128)S(1)} %get-tuple-element.77), channel_id=1, source_target_pairs={{16,0},{17,2},{22,4},{23,6},{26,8},{27,10},{28,12},{29,14},{2,16},... | collective-permute-start | bytes 165896 | tf_op jit(solution)/shard_map/ppermute | solution.py:189
  112.9 61.3 %copy-start.6 = (s32[1,13824]{1,0:T(1,128)}, s32[1,13824]{1,0:T(1,128)S(1)}, u32[]{:S(2)}) copy-start(s32[1,13824]{1,0:T(1,128)S(1)} %collective-permute-done.1) | copy-start | bytes 165892
  112.9 1.0 copy-start.1
  113.9 60.3 %collective-permute-start.4 = (s32[6,13824]{1,0:T(8,128)}, s32[6,13824]{1,0:T(8,128)}, u32[]{:S(2)}, u32[]{:S(2)}) collective-permute-start(s32[6,13824]{1,0:T(8,128)} %pad_add_fusion), channel_id=1, source_target_pairs={{0,1},{1,0},{2,3},{3,2},{4,5},{5,4},{6,7},{7,6},{8,9},{9,8},{10,11... | collective-permute-start | bytes 995336 | tf_op jit(solution)/shard_map/ppermute | solution.py:188
  171.7 11.4 %collective-permute-start.11 = (bf16[2,64,13824]{2,1,0:T(8,128)(2,1)S(1)}, bf16[2,64,13824]{2,1,0:T(8,128)(2,1)}, u32[]{:S(2)}, u32[]{:S(2)}) collective-permute-start(bf16[2,64,13824]{2,1,0:T(8,128)(2,1)S(1)} %copy-done), channel_id=1, source_target_pairs={{8,16},{12,20},{16,8},{20,12},{9,17},{13,21},{17,9},{21,13},{10,18... | collective-permute-start | bytes 10616840 | tf_op jit(solution)/shard_map/ppermute | solution.py:193
  174.2 80.1 %collective-permute-start.35 = (bf16[2,64,13824]{2,1,0:T(8,128)(2,1)}, bf16[2,64,13824]{2,1,0:T(8,128)(2,1)}, u32[]{:S(2)}, u32[]{:S(2)}) collective-permute-start(bf16[2,64,13824]{2,1,0:T(8,128)(2,1)} %collective-permute-done.6), channel_id=1, source_target_pairs={{0,4},{4,0},{8,12},{12,8},{16,20},{20,16},{24,28},{28,24},{1,5},{5... | collective-permute-start | bytes 10616840 | tf_op jit(solution)/shard_map/ppermute | solution.py:192
  176.7 80.2 %collective-permute-start.14 = (bf16[2,64,13824]{2,1,0:T(8,128)(2,1)}, bf16[2,64,13824]{2,1,0:T(8,128)(2,1)}, u32[]{:S(2)}, u32[]{:S(2)}) collective-permute-start(bf16[2,64,13824]{2,1,0:T(8,128)(2,1)} %collective-permute-done.6), channel_id=1, source_target_pairs={{0,8},{4,12},{8,0},{12,4},{16,24},{20,28},{24,16},{28,20},{1,9},{5... | collective-permute-start | bytes 10616840 | tf_op jit(solution)/shard_map/ppermute | solution.py:192
  178.4 79.7 %collective-permute-start.16 = (bf16[2,64,13824]{2,1,0:T(8,128)(2,1)}, bf16[2,64,13824]{2,1,0:T(8,128)(2,1)}, u32[]{:S(2)}, u32[]{:S(2)}) collective-permute-start(bf16[2,64,13824]{2,1,0:T(8,128)(2,1)} %collective-permute-done.6), channel_id=1, source_target_pairs={{8,16},{12,20},{16,8},{20,12},{9,17},{13,21},{17,9},{21,13},{10,18... | collective-permute-start | bytes 10616840 | tf_op jit(solution)/shard_map/ppermute | solution.py:193
  180.9 79.7 %collective-permute-start.8 = (bf16[2,64,13824]{2,1,0:T(8,128)(2,1)}, bf16[2,64,13824]{2,1,0:T(8,128)(2,1)}, u32[]{:S(2)}, u32[]{:S(2)}) collective-permute-start(bf16[2,64,13824]{2,1,0:T(8,128)(2,1)} %collective-permute-done.7), channel_id=1, source_target_pairs={{0,1},{1,0},{2,3},{3,2},{4,5},{5,4},{6,7},{7,6},{8,9},{9,8},{10,11... | collective-permute-start | bytes 10616840 | tf_op jit(solution)/shard_map/ppermute | solution.py:188
  183.1 146.9 %collective-permute-start.33 = (bf16[2,64,13824]{2,1,0:T(8,128)(2,1)S(1)}, bf16[2,64,13824]{2,1,0:T(8,128)(2,1)}, u32[]{:S(2)}, u32[]{:S(2)}) collective-permute-start(bf16[2,64,13824]{2,1,0:T(8,128)(2,1)S(1)} %copy-done), channel_id=1, source_target_pairs={{0,4},{4,0},{8,12},{12,8},{16,20},{20,16},{24,28},{28,24},{1,5},{5... | collective-permute-start | bytes 10616840 | tf_op jit(solution)/shard_map/ppermute | solution.py:192
  254.4 178.9 %collective-permute-start.10 = (bf16[2,64,13824]{2,1,0:T(8,128)(2,1)}, bf16[2,64,13824]{2,1,0:T(8,128)(2,1)}, u32[]{:S(2)}, u32[]{:S(2)}) collective-permute-start(bf16[2,64,13824]{2,1,0:T(8,128)(2,1)} %collective-permute-done.9), channel_id=1, source_target_pairs={{8,16},{12,20},{16,8},{20,12},{9,17},{13,21},{17,9},{21,13},{10,18... | collective-permute-start | bytes 10616840 | tf_op jit(solution)/shard_map/ppermute | solution.py:193
  256.8 178.9 %collective-permute-start.12 = (bf16[2,64,13824]{2,1,0:T(8,128)(2,1)}, bf16[2,64,13824]{2,1,0:T(8,128)(2,1)}, u32[]{:S(2)}, u32[]{:S(2)}) collective-permute-start(bf16[2,64,13824]{2,1,0:T(8,128)(2,1)} %collective-permute-done.11), channel_id=1, source_target_pairs={{8,0},{12,4},{16,24},{20,28},{9,1},{13,5},{17,25},{21,29},{10,2},{... | collective-permute-start | bytes 10616840 | tf_op jit(solution)/shard_map/ppermute | solution.py:193
  258.1 115.4 %collective-permute-start.15 = (bf16[2,64,13824]{2,1,0:T(8,128)(2,1)}, bf16[2,64,13824]{2,1,0:T(8,128)(2,1)}, u32[]{:S(2)}, u32[]{:S(2)}) collective-permute-start(bf16[2,64,13824]{2,1,0:T(8,128)(2,1)} %collective-permute-done.14), channel_id=1, source_target_pairs={{8,16},{12,20},{16,8},{20,12},{9,17},{13,21},{17,9},{21,13},{10,18... | collective-permute-start | bytes 10616840 | tf_op jit(solution)/shard_map/ppermute | solution.py:193
  260.6 157.9 %collective-permute-start.17 = (bf16[2,64,13824]{2,1,0:T(8,128)(2,1)}, bf16[2,64,13824]{2,1,0:T(8,128)(2,1)}, u32[]{:S(2)}, u32[]{:S(2)}) collective-permute-start(bf16[2,64,13824]{2,1,0:T(8,128)(2,1)} %collective-permute-done.16), channel_id=1, source_target_pairs={{8,0},{12,4},{16,24},{20,28},{9,1},{13,5},{17,25},{21,29},{10,2},{... | collective-permute-start | bytes 10616840 | tf_op jit(solution)/shard_map/ppermute | solution.py:193
  330.0 121.9 %collective-permute-start.37 = (f32[2,64,64]{2,1,0:T(8,128)}, f32[2,64,64]{2,1,0:T(8,128)S(1)}, u32[]{:S(2)}, u32[]{:S(2)}) collective-permute-start(f32[2,64,64]{2,1,0:T(8,128)} %get-tuple-element.71), channel_id=1, source_target_pairs={{0,2},{1,3},{2,0},{3,1},{4,6},{5,7},{6,4},{7,5},{8,10},{9,11},{10,... | collective-permute-start | bytes 98312 | tf_op jit(solution)/shard_map/ppermute | solution.py:188
  360.1 13.4 %copy-start.8 = (f32[2,64,64]{2,1,0:T(8,128)S(1)}, f32[2,64,64]{2,1,0:T(8,128)}, u32[]{:S(2)}) copy-start(f32[2,64,64]{2,1,0:T(8,128)} %get-tuple-element.72) | copy-start | bytes 98308
  373.5 78.5 %collective-permute-start.42 = (f32[2,64,64]{2,1,0:T(8,128)S(1)}, f32[2,64,64]{2,1,0:T(8,128)S(1)}, u32[]{:S(2)}, u32[]{:S(2)}) collective-permute-start(f32[2,64,64]{2,1,0:T(8,128)S(1)} %copy-done.8), channel_id=1, source_target_pairs={{0,1},{1,0},{2,3},{3,2},{4,5},{5,4},{6,7},{7,6},{8,9},{9,8},{10,11... | collective-permute-start | bytes 98312 | tf_op jit(solution)/shard_map/ppermute | solution.py:188
  418.4 34.2 %collective-permute-start.41 = (f32[2,64,64]{2,1,0:T(8,128)S(1)}, f32[2,64,64]{2,1,0:T(8,128)S(1)}, u32[]{:S(2)}, u32[]{:S(2)}) collective-permute-start(f32[2,64,64]{2,1,0:T(8,128)S(1)} %get-tuple-element.75), channel_id=1, source_target_pairs={{0,3},{1,2},{2,1},{3,0},{4,7},{5,6},{6,5},{7,4},{8,11},{9,10},{10,... | collective-permute-start | bytes 98312 | tf_op jit(solution)/shard_map/ppermute | solution.py:188
  418.8 16.9 %copy-start.7 = (f32[2,64,64]{2,1,0:T(8,128)S(1)}, f32[2,64,64]{2,1,0:T(8,128)}, u32[]{:S(2)}) copy-start(f32[2,64,64]{2,1,0:T(8,128)} %get-tuple-element.73) | copy-start | bytes 98308
  433.2 21.0 %collective-permute-start.40 = (f32[2,64,64]{2,1,0:T(8,128)S(1)}, f32[2,64,64]{2,1,0:T(8,128)S(1)}, u32[]{:S(2)}, u32[]{:S(2)}) collective-permute-start(f32[2,64,64]{2,1,0:T(8,128)S(1)} %get-tuple-element.76), channel_id=1, source_target_pairs={{0,2},{1,3},{2,0},{3,1},{4,6},{5,7},{6,4},{7,5},{8,10},{9,11},{10,... | collective-permute-start | bytes 98312 | tf_op jit(solution)/shard_map/ppermute | solution.py:188
  435.7 19.9 %collective-permute-start.39 = (f32[2,64,64]{2,1,0:T(8,128)S(1)}, f32[2,64,64]{2,1,0:T(8,128)S(1)}, u32[]{:S(2)}, u32[]{:S(2)}) collective-permute-start(f32[2,64,64]{2,1,0:T(8,128)S(1)} %copy-done.7), channel_id=1, source_target_pairs={{0,3},{1,2},{2,1},{3,0},{4,7},{5,6},{6,5},{7,4},{8,11},{9,10},{10,... | collective-permute-start | bytes 98312 | tf_op jit(solution)/shard_map/ppermute | solution.py:188
  437.1 14.7 %copy-start.3 = (f32[4,2,64,64]{3,2,1,0:T(8,128)S(1)}, f32[4,2,64,64]{3,2,1,0:T(8,128)}, u32[]{:S(2)}) copy-start(f32[4,2,64,64]{3,2,1,0:T(8,128)} %get-tuple-element.27) | copy-start | bytes 393220
  437.1 14.8 %copy-start.2 = (f32[4,2,64,64]{3,2,1,0:T(8,128)S(1)}, f32[4,2,64,64]{3,2,1,0:T(8,128)}, u32[]{:S(2)}) copy-start(f32[4,2,64,64]{3,2,1,0:T(8,128)} %get-tuple-element.25) | copy-start | bytes 393220
  437.1 14.9 %copy-start.12 = (f32[4,2,64,64]{3,2,1,0:T(8,128)S(1)}, f32[4,2,64,64]{3,2,1,0:T(8,128)}, u32[]{:S(2)}) copy-start(f32[4,2,64,64]{3,2,1,0:T(8,128)} %get-tuple-element.33) | copy-start | bytes 393220
  437.1 15.5 %copy-start.13 = (f32[4,2,64,64]{3,2,1,0:T(8,128)S(1)}, f32[4,2,64,64]{3,2,1,0:T(8,128)}, u32[]{:S(2)}) copy-start(f32[4,2,64,64]{3,2,1,0:T(8,128)} %get-tuple-element.31) | copy-start | bytes 393220
  437.2 26.0 %copy-start.11 = (f32[4,2,64,64]{3,2,1,0:T(8,128)S(1)}, f32[4,2,64,64]{3,2,1,0:T(8,128)}, u32[]{:S(2)}) copy-start(f32[4,2,64,64]{3,2,1,0:T(8,128)} %get-tuple-element.28) | copy-start | bytes 393220
  437.2 89.2 %copy-start.10 = (f32[4,2,64,64]{3,2,1,0:T(8,128)S(1)}, f32[4,2,64,64]{3,2,1,0:T(8,128)}, u32[]{:S(2)}) copy-start(f32[4,2,64,64]{3,2,1,0:T(8,128)} %get-tuple-element.26) | copy-start | bytes 393220
  437.2 98.3 %copy-start.9 = (f32[4,2,64,64]{3,2,1,0:T(8,128)S(1)}, f32[4,2,64,64]{3,2,1,0:T(8,128)}, u32[]{:S(2)}) copy-start(f32[4,2,64,64]{3,2,1,0:T(8,128)} %get-tuple-element.24) | copy-start | bytes 393220
  451.9 3.7 collective-permute-start.38
  452.0 75.0 %collective-permute-start.36 = (f32[4,2,64,64]{3,2,1,0:T(8,128)S(1)}, f32[4,2,64,64]{3,2,1,0:T(8,128)S(1)}, u32[]{:S(2)}, u32[]{:S(2)}) collective-permute-start(f32[4,2,64,64]{3,2,1,0:T(8,128)S(1)} %copy-done.12), channel_id=1, source_target_pairs={{0,6},{1,7},{2,4},{3,5},{4,2},{5,3},{6,0},{7,1},{8,14},{9,15},{10,... | collective-permute-start | bytes 393224 | tf_op jit(solution)/shard_map/ppermute | solution.py:189
  452.6 74.8 %collective-permute-start.34 = (f32[4,2,64,64]{3,2,1,0:T(8,128)S(1)}, f32[4,2,64,64]{3,2,1,0:T(8,128)S(1)}, u32[]{:S(2)}, u32[]{:S(2)}) collective-permute-start(f32[4,2,64,64]{3,2,1,0:T(8,128)S(1)} %copy-done.13), channel_id=1, source_target_pairs={{0,4},{1,5},{2,6},{3,7},{4,0},{5,1},{6,2},{7,3},{8,12},{9,13},{10,... | collective-permute-start | bytes 393224 | tf_op jit(solution)/shard_map/ppermute | solution.py:189
  454.3 8.9 %collective-permute-start.27 = (f32[2,64,64]{2,1,0:T(8,128)S(1)}, f32[2,64,64]{2,1,0:T(8,128)S(1)}, u32[]{:S(2)}, u32[]{:S(2)}) collective-permute-start(f32[2,64,64]{2,1,0:T(8,128)S(1)} %get-tuple-element.65), channel_id=1, source_target_pairs={{0,2},{1,3},{2,0},{3,1},{4,6},{5,7},{6,4},{7,5},{8,10},{9,11},{10,... | collective-permute-start | bytes 98312 | tf_op jit(solution)/shard_map/ppermute | solution.py:188
  455.6 70.8 %collective-permute-start.32 = (f32[2,64,64]{2,1,0:T(8,128)S(1)}, f32[2,64,64]{2,1,0:T(8,128)S(1)}, u32[]{:S(2)}, u32[]{:S(2)}) collective-permute-start(f32[2,64,64]{2,1,0:T(8,128)S(1)} %get-tuple-element.66), channel_id=1, source_target_pairs={{0,1},{1,0},{2,3},{3,2},{4,5},{5,4},{6,7},{7,6},{8,9},{9,8},{10,11... | collective-permute-start | bytes 98312 | tf_op jit(solution)/shard_map/ppermute | solution.py:188
  455.6 70.8 %collective-permute-start.31 = (f32[2,64,64]{2,1,0:T(8,128)S(1)}, f32[2,64,64]{2,1,0:T(8,128)S(1)}, u32[]{:S(2)}, u32[]{:S(2)}) collective-permute-start(f32[2,64,64]{2,1,0:T(8,128)S(1)} %get-tuple-element.69), channel_id=1, source_target_pairs={{0,3},{1,2},{2,1},{3,0},{4,7},{5,6},{6,5},{7,4},{8,11},{9,10},{10,... | collective-permute-start | bytes 98312 | tf_op jit(solution)/shard_map/ppermute | solution.py:188
  463.2 76.0 %collective-permute-start.26 = (f32[4,2,64,64]{3,2,1,0:T(8,128)S(1)}, f32[4,2,64,64]{3,2,1,0:T(8,128)S(1)}, u32[]{:S(2)}, u32[]{:S(2)}) collective-permute-start(f32[4,2,64,64]{3,2,1,0:T(8,128)S(1)} %copy-done.11), channel_id=1, source_target_pairs={{0,10},{1,11},{2,8},{3,9},{4,14},{5,15},{6,12},{7,13},{8,2},{9,3},... | collective-permute-start | bytes 393224 | tf_op jit(solution)/shard_map/ppermute | solution.py:189
  526.4 12.8 %collective-permute-start.25 = (f32[4,2,64,64]{3,2,1,0:T(8,128)S(1)}, f32[4,2,64,64]{3,2,1,0:T(8,128)S(1)}, u32[]{:S(2)}, u32[]{:S(2)}) collective-permute-start(f32[4,2,64,64]{3,2,1,0:T(8,128)S(1)} %copy-done.10), channel_id=1, source_target_pairs={{0,8},{1,9},{2,10},{3,11},{4,12},{5,13},{6,14},{7,15},{8,0},{9,1},... | collective-permute-start | bytes 393224 | tf_op jit(solution)/shard_map/ppermute | solution.py:189
  526.4 7.9 %collective-permute-start.30 = (f32[2,64,64]{2,1,0:T(8,128)S(1)}, f32[2,64,64]{2,1,0:T(8,128)S(1)}, u32[]{:S(2)}, u32[]{:S(2)}) collective-permute-start(f32[2,64,64]{2,1,0:T(8,128)S(1)} %get-tuple-element.70), channel_id=1, source_target_pairs={{0,2},{1,3},{2,0},{3,1},{4,6},{5,7},{6,4},{7,5},{8,10},{9,11},{10,... | collective-permute-start | bytes 98312 | tf_op jit(solution)/shard_map/ppermute | solution.py:188
  527.0 8.4 %collective-permute-start.29 = (f32[2,64,64]{2,1,0:T(8,128)S(1)}, f32[2,64,64]{2,1,0:T(8,128)S(1)}, u32[]{:S(2)}, u32[]{:S(2)}) collective-permute-start(f32[2,64,64]{2,1,0:T(8,128)S(1)} %get-tuple-element.67), channel_id=1, source_target_pairs={{0,3},{1,2},{2,1},{3,0},{4,7},{5,6},{6,5},{7,4},{8,11},{9,10},{10,... | collective-permute-start | bytes 98312 | tf_op jit(solution)/shard_map/ppermute | solution.py:188
  527.5 11.7 %collective-permute-start.28 = (f32[2,64,64]{2,1,0:T(8,128)S(1)}, f32[2,64,64]{2,1,0:T(8,128)S(1)}, u32[]{:S(2)}, u32[]{:S(2)}) collective-permute-start(f32[2,64,64]{2,1,0:T(8,128)S(1)} %get-tuple-element.68), channel_id=1, source_target_pairs={{0,1},{1,0},{2,3},{3,2},{4,5},{5,4},{6,7},{7,6},{8,9},{9,8},{10,11... | collective-permute-start | bytes 98312 | tf_op jit(solution)/shard_map/ppermute | solution.py:188
  534.3 6.8 %collective-permute-start.19 = (f32[2,64,64]{2,1,0:T(8,128)S(1)}, f32[2,64,64]{2,1,0:T(8,128)S(1)}, u32[]{:S(2)}, u32[]{:S(2)}) collective-permute-start(f32[2,64,64]{2,1,0:T(8,128)S(1)} %get-tuple-element.59), channel_id=1, source_target_pairs={{0,2},{1,3},{2,0},{3,1},{4,6},{5,7},{6,4},{7,5},{8,10},{9,11},{10,... | collective-permute-start | bytes 98312 | tf_op jit(solution)/shard_map/ppermute | solution.py:188
  535.5 22.2 %collective-permute-start.18 = (f32[4,2,64,64]{3,2,1,0:T(8,128)S(1)}, f32[4,2,64,64]{3,2,1,0:T(8,128)S(1)}, u32[]{:S(2)}, u32[]{:S(2)}) collective-permute-start(f32[4,2,64,64]{3,2,1,0:T(8,128)S(1)} %copy-done.9), channel_id=1, source_target_pairs={{0,18},{1,19},{2,16},{3,17},{4,22},{5,23},{6,20},{7,21},{8,26},{9,... | collective-permute-start | bytes 393224 | tf_op jit(solution)/shard_map/ppermute | solution.py:189
  539.1 22.5 %collective-permute-start.13 = (f32[4,2,64,64]{3,2,1,0:T(8,128)}, f32[4,2,64,64]{3,2,1,0:T(8,128)S(1)}, u32[]{:S(2)}, u32[]{:S(2)}) collective-permute-start(f32[4,2,64,64]{3,2,1,0:T(8,128)} %get-tuple-element.22), channel_id=1, source_target_pairs={{0,16},{1,17},{2,18},{3,19},{4,20},{5,21},{6,22},{7,23},{8,24},{9,... | collective-permute-start | bytes 393224 | tf_op jit(solution)/shard_map/ppermute | solution.py:189
  539.1 3.2 collective-permute-start.24
  539.2 3.8 collective-permute-start.23
  541.1 4.5 collective-permute-start.22
  542.4 4.4 collective-permute-start.21
  543.1 3.7 collective-permute-start.20
